TPU v7x, 32 devices: a whole 2x2x4 slice. The times are simulated.
32 devices in a mesh: row: 4 (over x, core), col: 8 (over z, y).
Axes of the slice: x: 2, y: 2, z: 4, core: 2. Of those that a mesh axis runs over, the one named last changes fastest.
Arguments:
- hidden: bfloat16 [128, 8192], P('col', 'row'), may hold values from -6 to 6
- w_gate: bfloat16 [8192, 16384], P('row', 'col'), may hold values from -0.0625 to 0.0625
- w_up: bfloat16 [8192, 16384], P('row', 'col'), may hold values from -0.0625 to 0.0625
- prior: float32 [16384, 16384], P('row', 'col'), may hold values from -1 to 12, as said below
- rhs: float32 [16384, 4096], P('row', 'col'), may hold values from -6 to 6
Outputs:
- factored: float32 [16384, 16384], P('row', 'col')
- right_out: float32 [16384, 4096], P('row', 'col')
Inputs may be any that keep to these rules, and one draw needn't show every extreme that they name: prior is symmetric and positive definite, with smallest eigenvalue 0.1 or more.
All inputs are finite; a program needn't handle non-finite values.
Results may differ from a plain program's by a relative error of at most 0.0003.
Values may be sent and summed in bfloat16 or wider, within the bound.
A program may use at most 192 MiB of HBM per device.

v0:
```python
import jax
import jax.numpy as jnp
from jax import lax
from jax.sharding import PartitionSpec as P

P_SIZE = 128
PANELS = 2


DAMP = 0.5


def from_root(value, axis, source):
    kept = jnp.where(lax.axis_index(axis) == source, value, 0).astype(value.dtype)
    return lax.psum(kept, axis)


def local(hidden, w_gate, w_up, prior, rhs):
    rows_count = lax.axis_size("row")
    cols_count = lax.axis_size("col")
    row_id = lax.axis_index("row")
    col_id = lax.axis_index("col")
    ratio = cols_count // rows_count
    height, width = prior.shape
    tokens = lax.all_gather(hidden, "col", axis=0, tiled=True)
    gate_part = jnp.dot(tokens, w_gate, preferred_element_type=jnp.float32)
    up_part = jnp.dot(tokens, w_up, preferred_element_type=jnp.float32)
    gate, upward = lax.psum((gate_part, up_part), "row")
    keys = jax.nn.silu(gate) * upward
    samples = keys.shape[0]
    regrouped = lax.all_to_all(keys, "col", split_axis=0, concat_axis=1, tiled=True)
    own_part = lax.dynamic_slice_in_dim(regrouped, row_id * height, height, 1)
    row_keys = lax.all_gather(own_part, "col", axis=0, tiled=True)
    row_global = row_id * height + lax.iota(jnp.int32, height)
    col_global = col_id * width + lax.iota(jnp.int32, width)
    outer = lax.dot_general(
        row_keys,
        keys,
        (((0,), (0,)), ((), ())),
        precision=lax.Precision.HIGHEST,
        preferred_element_type=jnp.float32,
    )
    work = prior + outer / samples
    work = work + jnp.where(row_global[:, None] == col_global[None, :], DAMP, 0.0).astype(
        jnp.float32
    )
    right = rhs
    offsets = lax.iota(jnp.int32, P_SIZE)
    for panel in range(PANELS):
        start = panel * P_SIZE
        stop = start + P_SIZE
        pivot = jnp.linalg.cholesky(work[start:stop, start:stop])
        pivot = from_root(pivot, "row", 0)
        column = work[:, start:stop]
        solved = jax.scipy.linalg.solve_triangular(pivot, column.T, lower=True).T
        placed = jnp.zeros_like(solved).at[start:stop].set(pivot)
        in_pivot = (row_global >= start) & (row_global < stop)
        beyond = row_global >= stop
        factor_cols = jnp.where(in_pivot[:, None], placed, jnp.where(beyond[:, None], solved, 0.0))
        factor_cols = from_root(factor_cols, "col", 0)
        matching = lax.dynamic_slice_in_dim(factor_cols, col_id % ratio * width, width, 0)
        across = from_root(matching, "row", col_id // ratio)
        lower_rows = jnp.where(beyond[:, None], factor_cols, 0.0)
        upper_cols = jnp.where((col_global >= stop)[:, None], across, 0.0)
        work = work - lax.dot_general(
            lower_rows,
            upper_cols,
            (((1,), (1,)), ((), ())),
            precision=lax.Precision.HIGHEST,
            preferred_element_type=jnp.float32,
        )
        solution = jax.scipy.linalg.solve_triangular(
            factor_cols[start:stop], right[start:stop], lower=True
        )
        solution = from_root(solution, "row", 0)
        right = right - jnp.dot(
            lower_rows,
            solution,
            precision=lax.Precision.HIGHEST,
            preferred_element_type=jnp.float32,
        )
        right = right.at[start:stop].set(jnp.where(row_id == 0, solution, right[start:stop]))
        keep_factor = (row_global[:, None] >= start + offsets[None, :]) & (col_id == 0)
        work = work.at[:, start:stop].set(jnp.where(keep_factor, factor_cols, work[:, start:stop]))
    return (work, right)


def solution(mesh):
    return jax.shard_map(
        local,
        mesh=mesh,
        in_specs=(
            P("col", "row"),
            P("row", "col"),
            P("row", "col"),
            P("row", "col"),
            P("row", "col"),
        ),
        out_specs=(P("row", "col"), P("row", "col")),
        check_vma=False,
    )
```

profile of v0, /device:TPU:0, one launch (start us, length us, event | category | flops | bytes accessed | tf_op | source)
XLA Modules:
  0.0 747.9 jit_solution(3485265117234313394)
XLA Ops:
  7.2 33.4 %all_gather.6 = bf16[128,2048]{1,0:T(8,128)(2,1)S(1)} all-gather(bf16[16,2048]{1,0:T(8,128)(2,1)} %param.22), channel_id=1, replica_groups=mesh['row'=4,'col'=8] {'col'}, dimensions={0}, use_global_device_ids=true | all-gather | bytes 589824 | tf_op jit(solution)/shard_map/all_gather | solution.py:25
  40.6 5.8 fusion.52
  48.7 52.7 %all-reduce.25.cloned.1.call-done = (f32[128,2048]{1,0:T(8,128)}, f32[128,2048]{1,0:T(8,128)}) async-done(((f32[128,2048]{1,0:T(8,128)}, f32[128,2048]{1,0:T(8,128)}), (f32[128,2048]{1,0:T(8,128)}, f32[128,2048]{1,0:T(8,128)})) %all-reduce.25.cloned.1.call-update) | async-done | bytes 2097168 | tf_op jit(solution)/shard_map/psum | solution.py:28
  109.7 25.6 %all-to-all-done = f32[8,16,2048]{2,1,0:T(8,128)S(1)} async-done(((f32[8,16,2048]{2,1,0:T(8,128)}), f32[8,16,2048]{2,1,0:T(8,128)S(1)}, u32[]{:S(2)}, u32[]{:S(2)}) %all-to-all-start) | async-done | bytes 1048608 | tf_op jit(solution)/shard_map/all_to_all | solution.py:31
  136.7 46.8 %all-gather.2.cloned.1.call-done = f32[128,4096]{1,0:T(8,128)} async-done(((f32[16,4096]{1,0:T(8,128)}), f32[128,4096]{1,0:T(8,128)}) %all-gather.2.cloned.1.call-update) | async-done | bytes 2097168 | tf_op jit(solution)/shard_map/all_gather | solution.py:33
  183.5 37.9 %select_add_fusion = f32[4096,2048]{1,0:T(8,128)} fusion(f32[4096,2048]{1,0:T(8,128)} %param.25, s32[2048]{0:T(1024)S(1)} %iota_add_fusion.1, s32[4096]{0:T(1024)S(1)} %iota_add_fusion, f32[128,4096]{1,0:T(8,128)} %all-gather.2.cloned.1.call-done, f32[128,2048]{1,0:T(8,128)} %multiply_multiply_fusion), kind=kOutput, calls=%fused_computation | convolution fusion | flops 12926844928 | bytes 70279168 | tf_op jit(solution)/shard_map/dot_general | solution.py:36
  223.3 11.7 %cholesky.44 = f32[128,128]{1,0:T(8,128)S(1)} custom-call(f32[128,128]{1,0:T(8,128)S(1)} %copy.22), custom_call_target="Cholesky" | custom-call | tf_op jit(solution)/shard_map/jit(cholesky)/cholesky | solution.py:52
  237.2 30.0 %all-reduce.13.cloned.1.call-done = f32[128,128]{1,0:T(8,128)} async-done(((f32[128,128]{1,0:T(8,128)}), f32[128,128]{1,0:T(8,128)}) %all-reduce.13.cloned.1.call-update) | async-done | bytes 65552 | tf_op jit(solution)/shard_map/psum | solution.py:15
  268.0 9.8 %custom-call.10 = f32[1,128,128]{1,2,0:T(8,128)S(1)} custom-call(f32[1,128,128]{2,1,0:T(8,128)S(1)} %select_bitcast_fusion.1), custom_call_target="InvertDiagBlocksLowerTriangular" | custom-call | tf_op jit(solution)/shard_map/jit(_solve_triangular)/triangular_solve | solution.py:55
  277.8 6.8 fusion.5
  285.4 101.7 %all-reduce.15.cloned.1.call-done = f32[4096,128]{1,0:T(8,128)} async-done(((f32[4096,128]{1,0:T(8,128)}), f32[4096,128]{1,0:T(8,128)}) %all-reduce.15.cloned.1.call-update) | async-done | bytes 2097168 | tf_op jit(solution)/shard_map/psum | solution.py:15
  389.6 9.8 %custom-call.12 = f32[1,128,128]{1,2,0:T(8,128)S(1)} custom-call(f32[1,128,128]{2,1,0:T(8,128)S(1)} %fusion.32), custom_call_target="InvertDiagBlocksLowerTriangular" | custom-call | tf_op jit(solution)/shard_map/jit(_solve_triangular)/triangular_solve | solution.py:72
  401.5 24.0 %all-reduce.17.cloned.1.call-done = f32[2048,128]{1,0:T(8,128)} async-done(((f32[2048,128]{1,0:T(8,128)}), f32[2048,128]{1,0:T(8,128)}) %all-reduce.17.cloned.1.call-update) | async-done | bytes 1048592 | tf_op jit(solution)/shard_map/psum | solution.py:15
  425.5 34.3 %convolution_subtract_fusion.1 = f32[4096,2048]{1,0:T(8,128)} fusion(f32[4096,2048]{1,0:T(8,128)} %select_add_fusion, f32[4096,128]{1,0:T(8,128)S(1)} %copy-done, f32[2048,128]{1,0:T(8,128)} %all-reduce.17.cloned.1.call-done, pred[4096]{0:T(1024)(128)(4,1)S(1)} %get-tuple-element.85, pred[2048]{0:T(1024)(128)(4,1)S(1)} %fusion.47), kind=kOutput, calls=%fused_computation.2 | convolution fusion | flops 12894076928 | bytes 70260736 | tf_op jit(solution)/shard_map/dot_general | solution.py:65
  466.9 11.7 %cholesky.55 = f32[128,128]{1,0:T(8,128)S(1)} custom-call(f32[128,128]{1,0:T(8,128)S(1)} %copy.25), custom_call_target="Cholesky" | custom-call | tf_op jit(solution)/shard_map/jit(cholesky)/cholesky | solution.py:52
  480.9 33.0 %all-reduce.23.cloned.1.call-done = (f32[128,128]{1,0:T(8,128)}, f32[128,512]{1,0:T(8,128)}) async-done(((f32[128,128]{1,0:T(8,128)}, f32[128,512]{1,0:T(8,128)}), (f32[128,128]{1,0:T(8,128)}, f32[128,512]{1,0:T(8,128)})) %all-reduce.23.cloned.1.call-update) | async-done | bytes 327696 | tf_op jit(solution)/shard_map/psum | solution.py:15
  514.7 9.8 %custom-call.11 = f32[1,128,128]{1,2,0:T(8,128)S(1)} custom-call(f32[1,128,128]{2,1,0:T(8,128)S(1)} %select_bitcast_fusion), custom_call_target="InvertDiagBlocksLowerTriangular" | custom-call | tf_op jit(solution)/shard_map/jit(_solve_triangular)/triangular_solve | solution.py:55
  524.5 6.9 fusion.2
  532.4 11.6 %convolution_subtract_fusion.3 = f32[4096,512]{1,0:T(8,128)} fusion(f32[4096,512]{1,0:T(8,128)} %param.26, f32[128,512]{1,0:T(8,128)S(1)} %copy-done.4, f32[4096,128]{1,0:T(8,128)S(1)} %copy-done, pred[4096]{0:T(1024)(128)(4,1)S(1)} %get-tuple-element.85), kind=kOutput, calls=%fused_computation.4 | convolution fusion | flops 3223846912 | bytes 19140608 | tf_op jit(solution)/shard_map/dot_general | solution.py:76
  545.7 88.2 %all-reduce.19.cloned.1.call-done = f32[4096,128]{1,0:T(8,128)} async-done(((f32[4096,128]{1,0:T(8,128)}), f32[4096,128]{1,0:T(8,128)}) %all-reduce.19.cloned.1.call-update) | async-done | bytes 2097168 | tf_op jit(solution)/shard_map/psum | solution.py:15
  634.9 9.8 %custom-call.13 = f32[1,128,128]{1,2,0:T(8,128)S(1)} custom-call(f32[1,128,128]{2,1,0:T(8,128)S(1)} %fusion.31), custom_call_target="InvertDiagBlocksLowerTriangular" | custom-call | tf_op jit(solution)/shard_map/jit(_solve_triangular)/triangular_solve | solution.py:72
  649.8 37.9 %all-reduce.21.cloned.1.call-done = (f32[2048,128]{1,0:T(8,128)}, f32[128,512]{1,0:T(8,128)}) async-done(((f32[2048,128]{1,0:T(8,128)}, f32[128,512]{1,0:T(8,128)}), (f32[2048,128]{1,0:T(8,128)}, f32[128,512]{1,0:T(8,128)})) %all-reduce.21.cloned.1.call-update) | async-done | bytes 1310736 | tf_op jit(solution)/shard_map/psum | solution.py:15
  687.7 9.8 %convolution_subtract_fusion.2 = f32[4096,512]{1,0:T(8,128)S(1)} fusion(f32[4096,512]{1,0:T(8,128)} %fusion.29, f32[128,512]{1,0:T(8,128)} %get-tuple-element.78, f32[4096,128]{1,0:T(8,128)S(1)} %copy-done.1, pred[4096]{0:T(1024)(128)(4,1)S(1)} %get-tuple-element.83), kind=kOutput, calls=%fused_computation.3 | convolution fusion | flops 3223846912 | bytes 19140608 | tf_op jit(solution)/shard_map/dot_general | solution.py:76
  697.5 37.9 %convolution_subtract_fusion = f32[4096,2048]{1,0:T(8,128)} fusion(f32[4096,2048]{1,0:T(8,128)} %fusion.6, f32[4096,128]{1,0:T(8,128)S(1)} %copy-done.1, f32[2048,128]{1,0:T(8,128)S(1)} %copy-done.3, pred[4096]{0:T(1024)(128)(4,1)S(1)} %get-tuple-element.83, pred[2048]{0:T(1024)(128)(4,1)S(1)} %fusion.46), kind=kOutput, calls=%fused_computation.1 | convolution fusion | flops 12894076928 | bytes 70260736 | tf_op jit(solution)/shard_map/dot_general | solution.py:65
  (73 shorter events, 46.3 us)
Async XLA Ops:
  7.2 94.2 %all-reduce.25.cloned.1.call-start = ((), (), s32[]{:S(2)}) async-start(), calls=%async_computation.8 | async-start | bytes 4194304 | tf_op jit(solution)/shard_map/psum | solution.py:28
  7.2 39.2 %slice-start = ((s8[8388608]{0:T(1024)(128)(4,1)}), s8[4194304]{0:T(1024)(128)(4,1)S(1)}, s32[]{:S(2)}) async-start(s8[8388608]{0:T(1024)(128)(4,1)} %bitcast.58), calls=%async_computation.9 | async-start | bytes 8388608
  40.6 5.8 slice-start.1
  104.1 31.1 %all-to-all-start = ((f32[8,16,2048]{2,1,0:T(8,128)}), f32[8,16,2048]{2,1,0:T(8,128)S(1)}, u32[]{:S(2)}, u32[]{:S(2)}) async-start(f32[8,16,2048]{2,1,0:T(8,128)} %bitcast), calls=%async_computation | async-start | bytes 2097152 | tf_op jit(solution)/shard_map/all_to_all | solution.py:31
  109.6 73.9 %all-gather.2.cloned.1.call-start = ((), (), s32[]{:S(2)}) async-start(), calls=%async_computation.1 | async-start | bytes 2359296 | tf_op jit(solution)/shard_map/all_gather | solution.py:33
  136.1 131.1 %all-reduce.13.cloned.1.call-start = ((), (), s32[]{:S(2)}) async-start(), calls=%async_computation.2 | async-start | bytes 131072 | tf_op jit(solution)/shard_map/psum | solution.py:15
  237.0 150.1 %all-reduce.15.cloned.1.call-start = ((), (), s32[]{:S(2)}) async-start(), calls=%async_computation.3 | async-start | bytes 4194304 | tf_op jit(solution)/shard_map/psum | solution.py:15
  284.6 140.9 %all-reduce.17.cloned.1.call-start = ((), (), s32[]{:S(2)}) async-start(), calls=%async_computation.4 | async-start | bytes 2097152 | tf_op jit(solution)/shard_map/psum | solution.py:15
  387.1 2.5 copy-start
  389.5 124.3 %all-reduce.23.cloned.1.call-start = ((), (), s32[]{:S(2)}) async-start(), calls=%async_computation.7 | async-start | bytes 655360 | tf_op jit(solution)/shard_map/psum | solution.py:15
  480.6 153.3 %all-reduce.19.cloned.1.call-start = ((), (), s32[]{:S(2)}) async-start(), calls=%async_computation.5 | async-start | bytes 4194304 | tf_op jit(solution)/shard_map/psum | solution.py:15
  531.4 0.9 copy-start.4
  531.4 156.2 %all-reduce.21.cloned.1.call-start = ((), (), s32[]{:S(2)}) async-start(), calls=%async_computation.6 | async-start | bytes 2621440 | tf_op jit(solution)/shard_map/psum | solution.py:15
  633.9 53.8 %copy-start.1 = (f32[4096,128]{1,0:T(8,128)S(1)}, f32[4096,128]{1,0:T(8,128)}, u32[]{:S(2)}) copy-start(f32[4096,128]{1,0:T(8,128)} %all-reduce.19.cloned.1.call-done) | copy-start | bytes 6291460
  687.7 9.8 %copy-start.5 = (f32[128,512]{1,0:T(8,128)S(1)}, f32[128,512]{1,0:T(8,128)}, u32[]{:S(2)}) copy-start(f32[128,512]{1,0:T(8,128)} %get-tuple-element.78) | copy-start | bytes 786436
  687.7 9.9 %copy-start.3 = (f32[2048,128]{1,0:T(8,128)S(1)}, f32[2048,128]{1,0:T(8,128)}, u32[]{:S(2)}) copy-start(f32[2048,128]{1,0:T(8,128)} %get-tuple-element.77) | copy-start | bytes 3145732
  697.5 37.9 %copy-start.2 = (f32[4096,512]{1,0:T(8,128)}, f32[4096,512]{1,0:T(8,128)S(1)}, u32[]{:S(2)}) copy-start(f32[4096,512]{1,0:T(8,128)S(1)} %fusion.27) | copy-start | bytes 25165828
Sparse Core Ops, SparseCore 0:
  48.8 52.4 all-reduce.24
  136.2 47.2 all-gather.1
  237.1 30.0 all-reduce.12
  284.8 102.2 all-reduce.14
  389.9 35.6 all-reduce.16
  480.7 33.0 all-reduce.22
  531.6 102.2 all-reduce.18
  649.2 38.3 all-reduce.20
where the time goes:
time: 752 us; the launch traced here: 748 us
  waiting for transfers between devices  440 us (59%)
  matrix products  157 us (21%)
  other arithmetic  91.9 us (12%)
  blocking collectives  33.4 us (4%)
  between operations  14.8 us (2%)
    psum x6, waiting for transfers between devices, from_root(): return lax.psum(kept, axis)  315 us
    dot_general x2, matrix products, local(): lax.dot_general(lower_rows, upper_cols, (((1,), (1,)), ((), ())), precisi...  72.1 us
    psum x1, waiting for transfers between devices, local(): gate, upward = lax.psum((gate_part, up_part), 'row')  52.7 us
    all_gather x1, waiting for transfers between devices, local(): row_keys = lax.all_gather(own_part, 'col', axis=0, tiled=True)  46.8 us
    dot_general x1, matrix products, local(): lax.dot_general(row_keys, keys, (((0,), (0,)), ((), ())), precision=lax.P...  37.9 us
    all_gather x1, blocking collectives, local(): tokens = lax.all_gather(hidden, 'col', axis=0, tiled=True)  33.4 us
    all_to_all x1, waiting for transfers between devices, local(): lax.all_to_all(keys, 'col', split_axis=0, concat_axis=1, tiled=True)  25.6 us
    another operation x6, other arithmetic, local(): pivot = jnp.linalg.cholesky(work[start:stop, start:stop])  24.8 us
  transfers between devices with their start and end apart: 9, of which 9 were waited for; matrix products, arithmetic and copies ran while one was open for 4% of the time, Pallas kernels for 0%

commit v1 on v0

v1 whole, which is shorter than its diff:
```python
import functools

import jax
import jax.numpy as jnp
from jax import lax
from jax.experimental import pallas as pl
from jax.experimental.pallas import tpu as pltpu
from jax.sharding import PartitionSpec as P

P_SIZE = 128
PANELS = 2
DAMP = 0.5
HIGH = lax.Precision.HIGHEST


def dot(a, b, dims=((1,), (0,))):
    return lax.dot_general(
        a, b, (dims, ((), ())), precision=HIGH, preferred_element_type=jnp.float32
    )


def split(value):
    high = lax.reduce_precision(value, 8, 7)
    return high.astype(jnp.bfloat16), (value - high).astype(jnp.bfloat16)


def eliminate(work, out):
    n = work.shape[0]
    lanes = lax.broadcasted_iota(jnp.int32, (n, n), 1)
    rows = lax.broadcasted_iota(jnp.int32, (n, 1), 0)

    def step(j, carry):
        row = work[pl.ds(j, 1), :]
        block = work[...]
        here = lanes == j
        column = jnp.sum(jnp.where(here, block[:, :n], 0.0), axis=1, keepdims=True)
        pivot = jnp.sum(jnp.where(here[:1], row[:, :n], 0.0), axis=1, keepdims=True)
        out[pl.ds(j, 1), :] = row / jnp.sqrt(pivot)
        work[...] = block - jnp.where(rows > j, column, 0.0) * (row / pivot)
        return carry

    lax.fori_loop(0, n, step, 0)


def inverse_kernel(a_ref, o_ref, work, out):
    size = a_ref.shape[0]
    n = P_SIZE
    eye = (
        lax.broadcasted_iota(jnp.int32, (n, n), 0)
        == lax.broadcasted_iota(jnp.int32, (n, n), 1)
    ).astype(jnp.float32)
    o_ref[...] = jnp.zeros_like(o_ref)
    for panel in range(size // n):
        c, e = panel * n, panel * n + n
        block = a_ref[c:e, c:e]
        if panel:
            left = dot(a_ref[c:e, :c], o_ref[:c, :c], ((1,), (1,)))
            block = block - dot(left, left, ((1,), (1,)))
        work[:, :n] = block
        work[:, n:] = eye
        eliminate(work, out)
        inverse = out[:, n:]
        o_ref[c:e, c:e] = inverse
        if panel:
            o_ref[c:e, :c] = -dot(inverse, dot(left, o_ref[:c, :c]))


def update_kernel(
    panels, at_ref, a_ref, b_ref, y_ref, yb_ref, factor_ref, prior_ref, rhs_ref, o_ref, r_ref
):
    tile, width = prior_ref.shape
    keyed = b_ref.shape[0] // 3 - panels
    row0 = at_ref[0] + pl.program_id(0) * tile
    col0 = at_ref[1]
    half = keyed + panels
    a = a_ref[...]
    high = a[:, half:]
    o_ref[...] = (
        prior_ref[...]
        + jnp.dot(a, b_ref[: 2 * half], preferred_element_type=jnp.float32)
        + jnp.dot(high, b_ref[2 * half :], preferred_element_type=jnp.float32)
    )
    r_ref[...] = (
        rhs_ref[...]
        + jnp.dot(a[:, keyed:half], yb_ref[:panels], preferred_element_type=jnp.float32)
        + jnp.dot(high[:, keyed:], yb_ref[:panels], preferred_element_type=jnp.float32)
        + jnp.dot(high[:, keyed:], yb_ref[panels:], preferred_element_type=jnp.float32)
    )

    @pl.when((row0 < col0 + width) & (col0 < row0 + tile))
    def _():
        start = pl.multiple_of(jnp.clip(row0 - col0, 0, width - tile), 128)
        rows = row0 + lax.broadcasted_iota(jnp.int32, (tile, tile), 0)
        cols = col0 + start + lax.broadcasted_iota(jnp.int32, (tile, tile), 1)
        there = o_ref[:, pl.ds(start, tile)]
        o_ref[:, pl.ds(start, tile)] = there + jnp.where(rows == cols, DAMP, 0.0)

    @pl.when(col0 == 0)
    def _():
        rows = row0 + lax.broadcasted_iota(jnp.int32, (tile, panels), 0)
        cols = lax.broadcasted_iota(jnp.int32, (tile, panels), 1)
        o_ref[:, :panels] = jnp.where(rows >= cols, factor_ref[...], o_ref[:, :panels])

    @pl.when(row0 == 0)
    def _():
        r_ref[:panels, :] = y_ref[...]


def local(hidden, w_gate, w_up, prior, rhs):
    rows_count = lax.axis_size("row")
    cols_count = lax.axis_size("col")
    row_id = lax.axis_index("row")
    col_id = lax.axis_index("col")
    ratio = cols_count // rows_count
    height, width = prior.shape
    wide = PANELS * P_SIZE
    columns = rhs.shape[1]
    first_row, first_col = row_id == 0, col_id == 0

    tokens = lax.all_gather(hidden, "col", axis=0, tiled=True)
    samples = tokens.shape[0]
    gate_part = jnp.dot(tokens, w_gate, preferred_element_type=jnp.float32)
    up_part = jnp.dot(tokens, w_up, preferred_element_type=jnp.float32)

    def keys_of(gate, up):
        return jax.nn.silu(gate) * up

    corner = jnp.where(first_row & first_col, prior[:wide, :wide], 0.0)
    pivots = jnp.concatenate([gate_part[:, :wide], up_part[:, :wide]], axis=0)
    pivots = jnp.concatenate([jnp.where(first_col, pivots, 0.0), corner], axis=0)
    pivots = lax.psum(pivots, ("row", "col"))
    pivot_keys = keys_of(pivots[:samples], pivots[samples : 2 * samples])
    index = lax.iota(jnp.int32, wide)
    eye = (index[:, None] == index[None, :]).astype(jnp.float32)
    pivot = (
        pivots[2 * samples :]
        + dot(pivot_keys, pivot_keys, ((0,), (0,))) / samples
        + DAMP * eye
    )
    inverse = pl.pallas_call(
        inverse_kernel,
        out_shape=jax.ShapeDtypeStruct((wide, wide), jnp.float32),
        scratch_shapes=[pltpu.VMEM((P_SIZE, 2 * P_SIZE), jnp.float32)] * 2,
    )(pivot)

    parts = jnp.stack([gate_part, up_part])
    parts = lax.psum_scatter(parts, "row", scatter_dimension=2, tiled=True)
    part_keys = keys_of(parts[0], parts[1])
    keys = lax.all_gather(part_keys, "row", axis=1, tiled=True)
    moves = [
        (r * cols_count + c, (c // ratio) * cols_count + (c % ratio) * rows_count + r)
        for r in range(rows_count)
        for c in range(cols_count)
    ]
    moved = lax.ppermute(part_keys, ("row", "col"), moves)
    row_keys_t = lax.all_gather(moved.T, "col", axis=0, tiled=True)

    late = part_keys[0, 0] * 0.0
    narrow = prior.at[:, :wide].get()
    prior_rows = jnp.where(first_col, narrow, 0.0).astype(jnp.bfloat16)
    prior_cols = jnp.where(first_row, prior[:wide], 0.0).astype(jnp.bfloat16)
    top = jnp.where(first_row, rhs[:wide], 0.0)
    prior_rows, prior_cols, top, _ = lax.optimization_barrier(
        (prior_rows, prior_cols, top, late)
    )
    prior_rows = lax.psum(prior_rows, "col").astype(jnp.float32)
    prior_cols = lax.psum(prior_cols, "row").astype(jnp.float32)
    top = lax.psum(top, "row")
    prior_rows = jnp.where(first_col, narrow, prior_rows)

    panel_rows = prior_rows + dot(row_keys_t, pivot_keys) / samples
    row_global = row_id * height + lax.iota(jnp.int32, height)
    col_global = col_id * width + lax.iota(jnp.int32, width)
    panel_rows = panel_rows + jnp.where(row_global[:, None] == index[None, :], DAMP, 0.0)
    factor_rows = dot(panel_rows, inverse, ((1,), (1,)))
    panel_cols = prior_cols + dot(pivot_keys, keys, ((0,), (0,))) / samples
    factor_cols = dot(inverse, panel_cols)
    solved = dot(inverse, top)

    stops = (index // P_SIZE + 1) * P_SIZE
    lower = jnp.where(row_global[:, None] >= stops[None, :], -factor_rows, 0.0)
    upper = jnp.where(col_global[None, :] >= stops[:, None], factor_cols, 0.0)
    rk_high, rk_low = split(row_keys_t)
    lo_high, lo_low = split(lower)
    ck_high, ck_low = split(keys / samples)
    up_high, up_low = split(upper)
    left = jnp.concatenate([rk_low, lo_low, rk_high, lo_high], axis=1)
    right = jnp.concatenate([ck_high, up_high, ck_high, up_high, ck_low, up_low], axis=0)
    solved_parts = jnp.concatenate(split(solved), axis=0)
    at = jnp.stack([row_id * height, col_id * width]).astype(jnp.int32)

    tile = min(512, height, width)
    by_row = lambda i, at: (i, 0)
    whole = lambda i, at: (0, 0)
    once = pl.Buffered(1)
    return pl.pallas_call(
        functools.partial(update_kernel, wide),
        grid_spec=pltpu.PrefetchScalarGridSpec(
            num_scalar_prefetch=1,
            grid=(height // tile,),
            in_specs=[
                pl.BlockSpec((tile, left.shape[1]), by_row),
                pl.BlockSpec(right.shape, whole, pipeline_mode=once),
                pl.BlockSpec(solved.shape, whole, pipeline_mode=once),
                pl.BlockSpec(solved_parts.shape, whole, pipeline_mode=once),
                pl.BlockSpec((tile, wide), by_row),
                pl.BlockSpec((tile, width), by_row),
                pl.BlockSpec((tile, columns), by_row),
            ],
            out_specs=[
                pl.BlockSpec((tile, width), by_row),
                pl.BlockSpec((tile, columns), by_row),
            ],
        ),
        out_shape=(
            jax.ShapeDtypeStruct(prior.shape, jnp.float32),
            jax.ShapeDtypeStruct(rhs.shape, jnp.float32),
        ),
        compiler_params=pltpu.CompilerParams(dimension_semantics=("arbitrary",)),
    )(at, left, right, solved, solved_parts, factor_rows, prior, rhs)


def solution(mesh):
    return jax.shard_map(
        local,
        mesh=mesh,
        in_specs=(
            P("col", "row"),
            P("row", "col"),
            P("row", "col"),
            P("row", "col"),
            P("row", "col"),
        ),
        out_specs=(P("row", "col"), P("row", "col")),
        check_vma=False,
    )
```

time: 752 us -> 506 us (0.67)
  matrix products: 157 us -> 29.4 us
  waiting for transfers between devices: 440 us -> 322 us
  Pallas kernels: 0 us -> 70.2 us
  other arithmetic: 91.9 us -> 28.2 us
    psum x7 -> x4, waiting for transfers between devices: 367 us -> 243 us  [the longest x1 105 us: local(): pivots = lax.psum(pivots, ('row', 'col'))]
    dot_general x5 -> x6, matrix products: 131 us -> 23.3 us  [dot(): lax.dot_general(a, b, (dims, ((), ())), precision=HIGH, preferred_element...]
    pallas_call x0 -> x2, Pallas kernels: none -> 70.2 us  [the longest x1 41.3 us: local(): pl.pallas_call(functools.partial(update_kernel, wide), grid_spec=pltpu.Pr...]
    another operation x16 -> x2, other arithmetic: 68.1 us -> 2.08 us  [the longest x1 1.46 us: local(): parts = jnp.stack([gate_part, up_part])]
    all_to_all x1 -> x0, waiting for transfers between devices: 25.6 us -> none  [local(): lax.all_to_all(keys, 'col', split_axis=0, concat_axis=1, tiled=True)]
    reduce_scatter x0 -> x1, waiting for transfers between devices: none -> 21.8 us  [local(): parts = lax.psum_scatter(parts, 'row', scatter_dimension=2, tiled=True)]
    another operation x4 -> x0, matrix products: 17.9 us -> none  [the longest x2 13.7 us: local(): solved = jax.scipy.linalg.solve_triangular(pivot, column.T, lower=True).T]
    scatter x4 -> x0, other arithmetic: 12.1 us -> none  [the longest x2 10.4 us: local(): work.at[:, start:stop]]
  transfers between devices with their start and end apart: 9 -> 8, of which waited for: 9 -> 7; matrix products, arithmetic and copies ran while one was open for 4% -> 8% of each run, Pallas kernels for 0% -> 6%
where the time goes in v1:
time: 506 us; the launch traced here: 505 us
  waiting for transfers between devices  322 us (64%)
  Pallas kernels  70.2 us (14%)
  blocking collectives  33.4 us (7%)
  matrix products  29.4 us (6%)
  other arithmetic  28.2 us (6%)
  between operations  15.7 us (3%)
    psum x1, waiting for transfers between devices, local(): pivots = lax.psum(pivots, ('row', 'col'))  105 us
    psum x1, waiting for transfers between devices, local(): prior_rows = lax.psum(prior_rows, 'col').astype(jnp.float32)  97.5 us
    pallas_call x1, Pallas kernels, local(): pl.pallas_call(functools.partial(update_kernel, wide), grid_spec=pltpu.Pr...  41.3 us
    all_gather x1, waiting for transfers between devices, local(): row_keys_t = lax.all_gather(moved.T, 'col', axis=0, tiled=True)  40.2 us
    psum x1, waiting for transfers between devices, local(): prior_cols = lax.psum(prior_cols, 'row').astype(jnp.float32)  36.9 us
    all_gather x1, blocking collectives, local(): tokens = lax.all_gather(hidden, 'col', axis=0, tiled=True)  33.4 us
    pallas_call x1, Pallas kernels, local(): pl.pallas_call(inverse_kernel, out_shape=jax.ShapeDtypeStruct((wide, wide...  28.9 us
    dot_general x6, matrix products, dot(): lax.dot_general(a, b, (dims, ((), ())), precision=HIGH, preferred_element...  23.3 us
  transfers between devices with their start and end apart: 8, of which 7 were waited for; matrix products, arithmetic and copies ran while one was open for 8% of the time, Pallas kernels for 6%

profile of v1, /device:TPU:0, one launch (start us, length us, event | category | flops | bytes accessed | tf_op | source)
XLA Modules:
  0.0 505.3 jit_solution(17582707548571765664)
XLA Ops:
  8.1 33.4 %all_gather.9 = bf16[128,2048]{1,0:T(8,128)(2,1)S(1)} all-gather(bf16[16,2048]{1,0:T(8,128)(2,1)} %param.5), channel_id=1, replica_groups=mesh['row'=4,'col'=8] {'col'}, dimensions={0}, use_global_device_ids=true | all-gather | bytes 589824 | tf_op jit(solution)/shard_map/all_gather | solution.py:120
  41.4 4.8 fusion.20
  51.1 3.9 select_convert_fusion
  55.0 2.9 select_convert_fusion.1
  57.9 1.9 slice_select_fusion
  59.9 21.8 %reduce-scatter.2.cloned.1.call-done = f32[2,128,512]{2,1,0:T(8,128)} async-done(((f32[2,128,2048]{2,1,0:T(8,128)}), f32[2,128,512]{2,1,0:T(8,128)}) %reduce-scatter.2.cloned.1.call-update) | async-done | bytes 524304 | tf_op jit(solution)/shard_map/reduce_scatter | solution.py:147
  88.1 105.3 %all-reduce.7.cloned.1.call-done = f32[512,256]{1,0:T(8,128)} async-done(((f32[512,256]{1,0:T(8,128)}), f32[512,256]{1,0:T(8,128)}) %all-reduce.7.cloned.1.call-update) | async-done | bytes 524304 | tf_op jit(solution)/shard_map/psum | solution.py:131
  193.3 2.4 fusion.7.a_ref
  195.7 28.9 %shard_map.68 = f32[256,256]{1,0:T(8,128)} custom-call(f32[256,256]{1,0:T(8,128)} %fusion.7.a_ref), custom_call_target="tpu_custom_call" | custom-call | tf_op jit(solution)/shard_map/pallas_call | solution.py:140
  224.6 3.4 all-reduce.11.cloned.1.call-done
  228.0 2.6 reduce-precision_convert_fusion.4
  231.4 15.4 %all-gather.5.cloned.1.call-done = f32[128,2048]{1,0:T(8,128)} async-done(((f32[128,512]{1,0:T(8,128)}), f32[128,2048]{1,0:T(8,128)}) %all-gather.5.cloned.1.call-update) | async-done | bytes 1048592 | tf_op jit(solution)/shard_map/all_gather | solution.py:149
  246.8 2.1 fusion.15
  248.9 36.9 %all-reduce.9.cloned.1.call-done = bf16[256,2048]{1,0:T(8,128)(2,1)} async-done(((bf16[256,2048]{1,0:T(8,128)(2,1)}), bf16[256,2048]{1,0:T(8,128)(2,1)}) %all-reduce.9.cloned.1.call-update) | async-done | bytes 1048592 | tf_op jit(solution)/shard_map/psum | solution.py:167
  285.8 3.6 fusion.3
  289.4 3.0 fusion.12
  296.7 40.2 %all-gather.3.cloned.1.call-done = f32[4096,128]{0,1:T(8,128)} async-done(((f32[512,128]{0,1:T(8,128)}), f32[4096,128]{0,1:T(8,128)}) %all-gather.3.cloned.1.call-update) | async-done | bytes 2097168 | tf_op jit(solution)/shard_map/all_gather | solution.py:156
  337.0 3.4 fusion.4
  342.0 2.3 copy.9
  344.2 97.5 %all-reduce.5.cloned.1.call-done = bf16[4096,256]{1,0:T(8,128)(2,1)} async-done(((bf16[4096,256]{1,0:T(8,128)(2,1)}), bf16[4096,256]{1,0:T(8,128)(2,1)}) %all-reduce.5.cloned.1.call-update) | async-done | bytes 2097168 | tf_op jit(solution)/shard_map/psum | solution.py:166
  441.7 6.4 %fusion.1 = f32[4096,256]{1,0:T(8,128)S(1)} fusion(f32[4096,128]{0,1:T(8,128)S(1)} %copy-done.1, bf16[4096,256]{1,0:T(8,128)(2,1)} %all-reduce.5.cloned.1.call-done, f32[4096,2048]{1,0:T(8,128)} %prior_ref.1, s32[4096]{0:T(1024)S(1)} %iota_add_fusion, pred[]{:T(512)S(6)} %eq.14, f32[512,256]{1,0:T(8,128)} %all-reduce.7.cloned.1.call-done), kind=kOutput, calls=%fused_computation.5 | convolution fusion | flops 1618116608 | bytes 12861441 | tf_op jit(solution)/shard_map/dot_general | solution.py:17
  448.1 5.4 %fusion.2 = (bf16[4096,256]{1,0:T(8,128)(2,1)S(1)}, bf16[4096,256]{1,0:T(8,128)(2,1)S(1)}, f32[4096,256]{1,0:T(8,128)}) fusion(s32[256]{0:T(256)S(1)} %fusion.18, s32[4096]{0:T(1024)S(1)} %iota_add_fusion, f32[4096,256]{1,0:T(8,128)S(1)} %fusion.1, f32[256,256]{1,0:T(8,128)S(1)} %copy-done.2), kind=kOutput, calls=%fused_computation.6 | convolution fusion | flops 3228565504 | bytes 12862464 | tf_op jit(solution)/shard_map/dot_general | solution.py:17
  453.5 3.1 pad_maximum_fusion.a_ref
  456.6 41.3 %shard_map.69 = (f32[4096,2048]{1,0:T(8,128)}, f32[4096,512]{1,0:T(8,128)}) custom-call(s32[2]{0:T(128)} %pad_add_fusion.at_ref, bf16[4096,768]{1,0:T(8,128)(2,1)} %pad_maximum_fusion.a_ref, bf16[1152,2048]{1,0:T(8,128)(2,1)} %fusion.9.b_ref, f32[256,512]{1,0:T(8,128)} %get-tuple-element.17.y_ref, bf16[512,512]{1,0:T(8,128)(2,1)} %pad_maximum_fusion.3.yb_ref, ...), custom_call_target="tpu_custom_call" | custom-call | tf_op jit(solution)/shard_map/pallas_call | solution.py:196
  (49 shorter events, 17.9 us)
Async XLA Ops:
  8.0 73.7 %reduce-scatter.2.cloned.1.call-start = ((), (), s32[]{:S(2)}) async-start(), calls=%async_computation.1 | async-start | bytes 2621440 | tf_op jit(solution)/shard_map/reduce_scatter | solution.py:147
  8.0 38.2 %slice-start = ((s8[8388608]{0:T(1024)(128)(4,1)}), s8[4194304]{0:T(1024)(128)(4,1)S(1)}, s32[]{:S(2)}) async-start(s8[8388608]{0:T(1024)(128)(4,1)} %bitcast.25), calls=%async_computation.8 | async-start | bytes 8388608
  41.4 4.8 slice-start.1
  49.1 144.3 %all-reduce.7.cloned.1.call-start = ((), (), s32[]{:S(2)}) async-start(), calls=%async_computation.4 | async-start | bytes 1048576 | tf_op jit(solution)/shard_map/psum | solution.py:131
  51.0 176.9 %all-reduce.11.cloned.1.call-start = ((), (), s32[]{:S(2)}) async-start(), calls=%async_computation.7 | async-start | bytes 1048576 | tf_op jit(solution)/shard_map/psum | solution.py:168
  59.8 186.9 %all-gather.5.cloned.1.call-start = ((), (), s32[]{:S(2)}) async-start(), calls=%async_computation.5 | async-start | bytes 1310720 | tf_op jit(solution)/shard_map/all_gather | solution.py:149
  83.5 202.2 %all-reduce.9.cloned.1.call-start = ((), (), s32[]{:S(2)}) async-start(), calls=%async_computation.6 | async-start | bytes 2097152 | tf_op jit(solution)/shard_map/psum | solution.py:167
  84.3 252.7 %all-gather.3.cloned.1.call-start = ((), (), s32[]{:S(2)}) async-start(), calls=%async_computation.2 | async-start | bytes 2359296 | tf_op jit(solution)/shard_map/all_gather | solution.py:156
  84.3 1.6 collective-permute-start
  85.9 0.7 copy-start.4
  86.7 355.0 %all-reduce.5.cloned.1.call-start = ((), (), s32[]{:S(2)}) async-start(), calls=%async_computation.3 | async-start | bytes 4194304 | tf_op jit(solution)/shard_map/psum | solution.py:166
  224.6 64.8 %copy-start.2 = (f32[256,256]{1,0:T(8,128)S(1)}, f32[256,256]{1,0:T(8,128)}, u32[]{:S(2)}) copy-start(f32[256,256]{1,0:T(8,128)} %shard_map.68) | copy-start | bytes 786436
  248.9 43.6 %copy-start = (f32[128,2048]{1,0:T(8,128)S(1)}, f32[128,2048]{1,0:T(8,128)}, u32[]{:S(2)}) copy-start(f32[128,2048]{1,0:T(8,128)} %all-gather.5.cloned.1.call-done) | copy-start | bytes 3145732
  337.0 104.8 %copy-start.1 = (f32[4096,128]{0,1:T(8,128)S(1)}, f32[4096,128]{0,1:T(8,128)}, u32[]{:S(2)}) copy-start(f32[4096,128]{0,1:T(8,128)} %all-gather.3.cloned.1.call-done) | copy-start | bytes 6291460
  448.1 5.4 %copy-start.3 = (bf16[4096,128]{1,0:T(8,128)(2,1)S(1)}, bf16[4096,128]{1,0:T(8,128)(2,1)}, u32[]{:S(2)}) copy-start(bf16[4096,128]{1,0:T(8,128)(2,1)} %copy.9) | copy-start | bytes 3145732
Sparse Core Ops, SparseCore 0:
  49.2 32.4 reduce-scatter.1
Sparse Core Ops, SparseCore 1:
  54.8 138.5 all-reduce.6
  195.6 32.4 all-reduce.10
  230.0 16.7 all-gather.4
  249.2 36.5 all-reduce.8
  288.0 48.9 all-gather.2
  341.2 100.5 all-reduce.4
